TPU v7x, 256 devices: a whole 4x4x8 slice. The times are simulated.
256 devices in a mesh: depth: 8 (over y, x_lo), tile: 32 (over z, x_hi, core).
Axes of the slice: x: 4 (x_hi: 2, x_lo: 2; x = x_hi * 2 + x_lo), y: 4, z: 8, core: 2. Of those that a mesh axis runs over, the one named last changes fastest.
Arguments:
- warm_field: float32 [16, 2, 16, 256, 256], P(None, None, 'depth', 'tile'), may hold values from -6 to 6
- slowness_sq: float32 [16, 256, 256], P('depth', 'tile'), may hold values from 1.2 to 2.6
- adjoint_field: float32 [16, 2, 16, 256, 256], P(None, None, 'depth', 'tile'), may hold values from -6 to 6
- observed: float32 [16, 2, 256], replicated, may hold values from -6 to 6
- source_cell: int32 [16], replicated, may hold values from 0 to 1048575
- receiver_cell: int32 [16, 256], replicated, may hold values from 0 to 1048575
- pml_width: int32 [4], replicated, may hold values from 2 to 4
Outputs:
- new_field: float32 [16, 2, 16, 256, 256], P(None, None, 'depth', 'tile')
- misfit: float32 [16], replicated
- gradient: float32 [16, 256, 256], P('depth', 'tile')
All inputs are finite; a program needn't handle non-finite values.
Results may differ from a plain program's by a relative error of at most 0.00002.
Values sent between devices are 32-bit elements; how exact they have to be, the bound alone decides.
A program may use at most 64 MiB of HBM per device.

v0:
```python
import jax
import jax.numpy as jnp
from jax import lax
from jax.sharding import PartitionSpec as P

WAVE_SCALE = 1.9
PML_DAMP = 2.0
SOURCE_AMPLITUDE = 25.0
SHIFT_IMAG = 0.5
CENTER_WEIGHT = 128.0 / 30.0
LUMPED_DIAG = 2.0
LAP_WEIGHTS = (0.0, 14.0 / 30.0, 3.0 / 30.0, 1.0 / 30.0)
MASS_WEIGHTS = (1.0 / 6.0, 2.0 / 3.0, 1.0 / 6.0)


def extended(shard, sides, width):
    for axis, dim in sides:
        size, length = (lax.axis_size(axis), shard.shape[dim])
        up = [(i, (i + 1) % size) for i in range(size - 1)]
        down = [(j, i) for i, j in up]
        last = lax.slice_in_dim(shard, length - width, length, axis=dim)
        leading = lax.slice_in_dim(shard, 0, width, axis=dim)
        before = lax.ppermute(last, axis, up)
        after = lax.ppermute(leading, axis, down)
        shard = jnp.concatenate([before, shard, after], axis=dim)
    return shard


def shifted(value, axis, steps):
    count = lax.axis_size(axis)
    leading, last = (max(0, -steps), min(count, count - steps))
    return lax.ppermute(value, axis, [(source, source + steps) for source in range(leading, last)])


def damping_ramp(distance, extent):
    fraction = jnp.maximum((extent - distance) / extent, 0.0)
    return fraction * fraction


def damping_field(pml_width, depth_pos, width_pos, full_depth, full_width):
    widths = pml_width.astype(jnp.float32)
    depth_part = damping_ramp(depth_pos, widths[0]) + damping_ramp(
        full_depth - 1.0 - depth_pos, widths[1]
    )
    width_part = damping_ramp(width_pos, widths[2]) + damping_ramp(
        full_width - 1.0 - width_pos, widths[3]
    )
    return PML_DAMP * (depth_part[:, None] + width_part[None, :])


def pad_long(values):
    return jnp.pad(values, [(0, 0)] * (values.ndim - 1) + [(1, 1)])


def laplacian_from_padded(padded, depth_len, width_len, long_len):
    summed = CENTER_WEIGHT * padded[..., 1 : 1 + depth_len, 1 : 1 + width_len, 1 : 1 + long_len]
    for off_depth in (-1, 0, 1):
        for off_width in (-1, 0, 1):
            for off_long in (-1, 0, 1):
                order_no = abs(off_depth) + abs(off_width) + abs(off_long)
                if order_no > 0:
                    summed = (
                        summed
                        - LAP_WEIGHTS[order_no]
                        * padded[
                            ...,
                            1 + off_depth : 1 + off_depth + depth_len,
                            1 + off_width : 1 + off_width + width_len,
                            1 + off_long : 1 + off_long + long_len,
                        ]
                    )
    return summed


def lateral_smooth(padded, width_len, long_len):
    summed = None
    for off_width in range(3):
        for off_long in range(3):
            weighted = (
                MASS_WEIGHTS[off_width]
                * MASS_WEIGHTS[off_long]
                * padded[..., off_width : off_width + width_len, off_long : off_long + long_len]
            )
            summed = weighted if summed is None else summed + weighted
    return summed


def plane_coupling(padded, width_len, long_len):
    summed = None
    for off_width in range(3):
        for off_long in range(3):
            order_no = 1 + (off_width != 1) + (off_long != 1)
            weighted = (
                LAP_WEIGHTS[order_no]
                * padded[..., off_width : off_width + width_len, off_long : off_long + long_len]
            )
            summed = weighted if summed is None else summed + weighted
    return summed


def combine_operator(negative, mass, damping):
    real_out = negative[:, 0] - WAVE_SCALE * (mass[:, 0] - damping * mass[:, 1])
    imag_out = negative[:, 1] - WAVE_SCALE * (mass[:, 1] + damping * mass[:, 0])
    return jnp.stack([real_out, imag_out], axis=1)


def inverse_diagonal(slowness, damping):
    scaled = WAVE_SCALE * MASS_WEIGHTS[1] * MASS_WEIGHTS[1] * slowness
    diag_re = LUMPED_DIAG - scaled * (1.0 + SHIFT_IMAG * damping)
    diag_im = -scaled * (damping + SHIFT_IMAG)
    norm_sq = diag_re * diag_re + diag_im * diag_im
    return (diag_re / norm_sq, -diag_im / norm_sq)


def complex_scale(inv_re, inv_im, values):
    real_part = values[:, 0]
    imag_part = values[:, 1]
    return jnp.stack(
        [inv_re * real_part - inv_im * imag_part, inv_re * imag_part + inv_im * real_part], axis=1
    )


def per_device(
    warm_field, slowness_sq, adjoint_field, observed, source_cell, receiver_cell, pml_width
):
    shot_count, _, layer_len, width_len, long_len = warm_field.shape
    depth_index = lax.axis_index("depth")
    tile_index = lax.axis_index("tile")
    depth_count = lax.axis_size("depth")
    tile_count = lax.axis_size("tile")
    full_depth = layer_len * depth_count
    full_width = width_len * tile_count
    depth_cells = depth_index * layer_len + jnp.arange(layer_len, dtype=jnp.int32)
    width_cells = tile_index * width_len + jnp.arange(width_len, dtype=jnp.int32)
    width_wide = (tile_index * width_len - 1 + jnp.arange(width_len + 2, dtype=jnp.int32)).astype(
        jnp.float32
    )
    damping_wide = damping_field(
        pml_width, depth_cells.astype(jnp.float32), width_wide, full_depth * 1.0, full_width * 1.0
    )[:, :, None]
    damping = damping_wide[:, 1:-1]
    slowness_wide = extended(slowness_sq, (("tile", 1),), 1)

    def apply_operator(values):
        padded = extended(values, (("depth", 2), ("tile", 3)), 1)
        negative = laplacian_from_padded(pad_long(padded), layer_len, width_len, long_len)
        mass = lateral_smooth(pad_long(padded[:, :, 1:-1] * slowness_wide), width_len, long_len)
        return combine_operator(negative, mass, damping)

    cell_index = (
        depth_cells[:, None, None] * full_width + width_cells[None, :, None]
    ) * long_len + jnp.arange(long_len, dtype=jnp.int32)[None, None, :]
    hits = cell_index[None] == source_cell[:, None, None, None]
    source_re = jnp.where(hits, SOURCE_AMPLITUDE, 0.0).astype(jnp.float32)
    forcing = jnp.stack([source_re, jnp.zeros_like(source_re)], axis=1)
    residual = forcing - apply_operator(warm_field)
    inv_re, inv_im = inverse_diagonal(slowness_sq, damping)

    def couple(plane_in):
        with_rims = extended(plane_in, (("tile", 2),), 1)
        return plane_coupling(pad_long(with_rims), width_len, long_len)

    def down_section(source_part, incoming):
        previous = incoming
        layers_out = []
        for layer_no in range(layer_len):
            source_term = source_part[:, :, layer_no] + couple(previous)
            previous = complex_scale(inv_re[layer_no], inv_im[layer_no], source_term)
            layers_out.append(previous)
        return jnp.stack(layers_out, axis=2)

    def up_section(downward_part, incoming):
        previous = incoming
        layers_out = [None] * layer_len
        for layer_no in range(layer_len - 1, -1, -1):
            previous = downward_part[:, :, layer_no] + complex_scale(
                inv_re[layer_no], inv_im[layer_no], couple(previous)
            )
            layers_out[layer_no] = previous
        return jnp.stack(layers_out, axis=2)

    groups = 1
    per_group = shot_count // groups

    def run_chain(inputs, downward):
        position = depth_index if downward else depth_count - 1 - depth_index

        def segment_body(segment_no, state_pair):
            result, outgoing = state_pair
            if downward:
                incoming = shifted(outgoing, "depth", 1)
            else:
                incoming = shifted(outgoing, "depth", -1)
            group_no = segment_no - position
            is_valid = jnp.logical_and(group_no >= 0, group_no < groups)
            group_start = jnp.clip(group_no, 0, groups - 1) * per_group
            if downward:
                updated = down_section(inputs, incoming)
                edge_plane = updated[:, :, layer_len - 1]
            else:
                updated = up_section(inputs, incoming)
                edge_plane = updated[:, :, 0]
            current = result
            result = lax.dynamic_update_slice_in_dim(
                result, jnp.where(is_valid, updated, current), group_start, 0
            )
            outgoing = jnp.where(is_valid, edge_plane, outgoing)
            return (result, outgoing)

        initial = (
            jnp.zeros_like(inputs),
            jnp.zeros((per_group, 2, width_len, long_len), jnp.float32),
        )
        final_pair = lax.fori_loop(0, depth_count + groups - 1, segment_body, initial)
        return final_pair[0]

    downward = run_chain(residual, True)
    search = run_chain(downward, False)
    image_field = apply_operator(search)
    local_real = jnp.sum(
        image_field[:, 0] * residual[:, 0] + image_field[:, 1] * residual[:, 1], axis=(1, 2, 3)
    )
    local_imag = jnp.sum(
        image_field[:, 0] * residual[:, 1] - image_field[:, 1] * residual[:, 0], axis=(1, 2, 3)
    )
    local_norm = jnp.sum(
        image_field[:, 0] * image_field[:, 0] + image_field[:, 1] * image_field[:, 1],
        axis=(1, 2, 3),
    )
    plane_cells = full_width * long_len
    rec_depth = receiver_cell // plane_cells
    rec_width = receiver_cell // long_len % full_width
    rec_long = receiver_cell % long_len
    local_depth = rec_depth - depth_index * layer_len
    local_width = rec_width - tile_index * width_len
    is_owned = (
        (local_depth >= 0)
        & (local_depth < layer_len)
        & (local_width >= 0)
        & (local_width < width_len)
    )
    row_count = layer_len * width_len
    local_row = jnp.where(is_owned, local_depth * width_len + local_width, -1)
    row_hot = (local_row[:, :, None] == jnp.arange(row_count, dtype=jnp.int32)).astype(jnp.float32)
    both_fields = jnp.concatenate([warm_field, search], axis=1).reshape(
        shot_count, 4, row_count, long_len
    )
    picked_rows = jnp.einsum(
        "srk,sqky->sqry", row_hot, both_fields, precision=lax.Precision.HIGHEST
    )
    col_hot = rec_long[:, None, :, None] == jnp.arange(long_len, dtype=jnp.int32)
    picked = jnp.sum(jnp.where(col_hot, picked_rows, 0.0), axis=-1)
    packed = jnp.concatenate(
        [jnp.stack([local_real, local_imag, local_norm], axis=1), picked.reshape(shot_count, -1)],
        axis=1,
    )
    packed = lax.psum(packed, ("depth", "tile"))
    dot_real, dot_imag, image_norm = (packed[:, 0], packed[:, 1], packed[:, 2])
    picked = packed[:, 3:].reshape(shot_count, 4, -1)
    step_re = (dot_real / image_norm)[:, None, None, None]
    step_im = (dot_imag / image_norm)[:, None, None, None]
    new_re = warm_field[:, 0] + step_re * search[:, 0] - step_im * search[:, 1]
    new_im = warm_field[:, 1] + step_re * search[:, 1] + step_im * search[:, 0]
    new_field = jnp.stack([new_re, new_im], axis=1)
    rec_re = (dot_real / image_norm)[:, None]
    rec_im = (dot_imag / image_norm)[:, None]
    sampled_re = picked[:, 0] + rec_re * picked[:, 2] - rec_im * picked[:, 3]
    sampled_im = picked[:, 1] + rec_re * picked[:, 3] + rec_im * picked[:, 2]
    miss_re = sampled_re - observed[:, 0]
    miss_im = sampled_im - observed[:, 1]
    misfit = 0.5 * jnp.sum(miss_re * miss_re + miss_im * miss_im, axis=1)
    adjoint_wide = extended(adjoint_field, (("tile", 3),), 1)
    adjoint_re = adjoint_wide[:, 0]
    adjoint_im = adjoint_wide[:, 1]
    weight_re = adjoint_re + damping_wide * adjoint_im
    weight_im = damping_wide * adjoint_re - adjoint_im
    smooth_re = lateral_smooth(pad_long(weight_re), width_len, long_len)
    smooth_im = lateral_smooth(pad_long(weight_im), width_len, long_len)
    gradient = -WAVE_SCALE / shot_count * jnp.sum(new_re * smooth_re - new_im * smooth_im, axis=0)
    return (new_field, misfit, gradient)


def solution(mesh):
    return jax.shard_map(
        per_device,
        mesh=mesh,
        in_specs=(
            P(None, None, "depth", "tile", None),
            P("depth", "tile", None),
            P(None, None, "depth", "tile", None),
            P(),
            P(),
            P(),
            P(),
        ),
        out_specs=(P(None, None, "depth", "tile", None), P(), P("depth", "tile", None)),
        check_vma=False,
    )
```

profile of v0, /device:TPU:1, one launch (start us, length us, event | category | flops | bytes accessed | tf_op | source)
XLA Modules:
  0.0 895.7 jit_solution(5374901224782929633)
XLA Ops:
  8.4 3.9 collective-permute-start.10
  14.4 5.2 collective-permute-start.14
  32.3 5.1 collective-permute-start.12
  40.9 5.1 collective-permute-start.20
  50.7 3.6 fusion.119
  54.6 255.1 %while.36 = (s32[]{:T(128)}, f32[16,2,2,8,256]{4,3,2,1,0:T(8,128)S(1)}, f32[16,2,8,256]{3,2,1,0:T(8,128)S(1)}, s32[]{:T(128)}, f32[2,8,256]{2,1,0:T(8,128)S(1)},...) while((s32[]{:T(128)}, ...), condition=%wide.region_1.2_spmd.clone, body=%wide.region_0.1_spmd.clone.sunk | while | flops 5369095 | bytes 13800788 | solution.py:214
  54.7 3.7 collective-permute-start
  58.4 3.8 collective-permute-done
  64.1 8.4 collective-permute-start.2
  77.1 5.8 collective-permute-start.4
  85.2 3.7 collective-permute-start
  88.9 3.3 collective-permute-done
  94.1 9.8 %collective-permute-start.2 = (f32[16,2,1,256]{3,2,1,0:T(1,128)S(1)}, f32[16,2,1,256]{3,2,1,0:T(1,128)S(1)}, u32[]{:S(2)}, u32[]{:S(2)}) collective-permute-start(f32[16,2,1,256]{3,2,1,0:T(1,128)S(1)} %get-tuple-element.707), channel_id=1, source_target_pairs={{0,1},{1,2},{2,3},{3,4},{4,5},{5,6},{6,7},{7,8},{8,9},{9,10},{10,1... | collective-permute-start | bytes 98312 | tf_op jit(solution)/shard_map/while/body/eval_jaxpr/ppermute | solution.py:23
  108.4 5.7 collective-permute-start.4
  116.4 4.8 collective-permute-start
  126.5 9.8 %collective-permute-start.2 = (f32[16,2,1,256]{3,2,1,0:T(1,128)S(1)}, f32[16,2,1,256]{3,2,1,0:T(1,128)S(1)}, u32[]{:S(2)}, u32[]{:S(2)}) collective-permute-start(f32[16,2,1,256]{3,2,1,0:T(1,128)S(1)} %get-tuple-element.707), channel_id=1, source_target_pairs={{0,1},{1,2},{2,3},{3,4},{4,5},{5,6},{6,7},{7,8},{8,9},{9,10},{10,1... | collective-permute-start | bytes 98312 | tf_op jit(solution)/shard_map/while/body/eval_jaxpr/ppermute | solution.py:23
  140.8 5.7 collective-permute-start.4
  149.0 4.4 collective-permute-start
  153.4 3.3 collective-permute-done
  158.6 9.8 %collective-permute-start.2 = (f32[16,2,1,256]{3,2,1,0:T(1,128)S(1)}, f32[16,2,1,256]{3,2,1,0:T(1,128)S(1)}, u32[]{:S(2)}, u32[]{:S(2)}) collective-permute-start(f32[16,2,1,256]{3,2,1,0:T(1,128)S(1)} %get-tuple-element.707), channel_id=1, source_target_pairs={{0,1},{1,2},{2,3},{3,4},{4,5},{5,6},{6,7},{7,8},{8,9},{9,10},{10,1... | collective-permute-start | bytes 98312 | tf_op jit(solution)/shard_map/while/body/eval_jaxpr/ppermute | solution.py:23
  173.0 5.7 collective-permute-start.4
  181.2 4.4 collective-permute-start
  185.6 3.3 collective-permute-done
  190.8 9.8 %collective-permute-start.2 = (f32[16,2,1,256]{3,2,1,0:T(1,128)S(1)}, f32[16,2,1,256]{3,2,1,0:T(1,128)S(1)}, u32[]{:S(2)}, u32[]{:S(2)}) collective-permute-start(f32[16,2,1,256]{3,2,1,0:T(1,128)S(1)} %get-tuple-element.707), channel_id=1, source_target_pairs={{0,1},{1,2},{2,3},{3,4},{4,5},{5,6},{6,7},{7,8},{8,9},{9,10},{10,1... | collective-permute-start | bytes 98312 | tf_op jit(solution)/shard_map/while/body/eval_jaxpr/ppermute | solution.py:23
  205.2 5.7 collective-permute-start.4
  213.4 4.4 collective-permute-start
  223.0 9.8 %collective-permute-start.2 = (f32[16,2,1,256]{3,2,1,0:T(1,128)S(1)}, f32[16,2,1,256]{3,2,1,0:T(1,128)S(1)}, u32[]{:S(2)}, u32[]{:S(2)}) collective-permute-start(f32[16,2,1,256]{3,2,1,0:T(1,128)S(1)} %get-tuple-element.707), channel_id=1, source_target_pairs={{0,1},{1,2},{2,3},{3,4},{4,5},{5,6},{6,7},{7,8},{8,9},{9,10},{10,1... | collective-permute-start | bytes 98312 | tf_op jit(solution)/shard_map/while/body/eval_jaxpr/ppermute | solution.py:23
  237.4 5.7 collective-permute-start.4
  245.6 4.4 collective-permute-start
  255.3 9.8 %collective-permute-start.2 = (f32[16,2,1,256]{3,2,1,0:T(1,128)S(1)}, f32[16,2,1,256]{3,2,1,0:T(1,128)S(1)}, u32[]{:S(2)}, u32[]{:S(2)}) collective-permute-start(f32[16,2,1,256]{3,2,1,0:T(1,128)S(1)} %get-tuple-element.707), channel_id=1, source_target_pairs={{0,1},{1,2},{2,3},{3,4},{4,5},{5,6},{6,7},{7,8},{8,9},{9,10},{10,1... | collective-permute-start | bytes 98312 | tf_op jit(solution)/shard_map/while/body/eval_jaxpr/ppermute | solution.py:23
  269.6 5.7 collective-permute-start.4
  277.8 4.4 collective-permute-start
  287.5 9.8 %collective-permute-start.2 = (f32[16,2,1,256]{3,2,1,0:T(1,128)S(1)}, f32[16,2,1,256]{3,2,1,0:T(1,128)S(1)}, u32[]{:S(2)}, u32[]{:S(2)}) collective-permute-start(f32[16,2,1,256]{3,2,1,0:T(1,128)S(1)} %get-tuple-element.707), channel_id=1, source_target_pairs={{0,1},{1,2},{2,3},{3,4},{4,5},{5,6},{6,7},{7,8},{8,9},{9,10},{10,1... | collective-permute-start | bytes 98312 | tf_op jit(solution)/shard_map/while/body/eval_jaxpr/ppermute | solution.py:23
  301.8 5.7 collective-permute-start.4
  309.8 256.7 %while.37 = (s32[]{:T(128)}, f32[16,2,2,8,256]{4,3,2,1,0:T(8,128)S(1)}, f32[16,2,8,256]{3,2,0,1:T(8,128)S(1)}, s32[]{:T(128)}, f32[16,2,2,8,256]{4,3,0,1,2:T(8,1...) while((s32[]{:T(128)}, ...), condition=%wide.region_3.4_spmd.clone, body=%wide.region_2.3_spmd.clone.sunk | while | flops 5318663 | bytes 15177044 | solution.py:214
  311.2 6.9 collective-permute-done.5
  320.0 10.3 %collective-permute-start.7 = (f32[16,2,1,256]{3,2,0,1:T(1,128)S(1)}, f32[16,2,1,256]{3,2,0,1:T(1,128)S(1)}, u32[]{:S(2)}, u32[]{:S(2)}) collective-permute-start(f32[16,2,1,256]{3,2,0,1:T(1,128)S(1)} %get-tuple-element.730), channel_id=1, source_target_pairs={{0,1},{1,2},{2,3},{3,4},{4,5},{5,6},{6,7},{7,8},{8,9},{9,10},{10,1... | collective-permute-start | bytes 98312 | tf_op jit(solution)/shard_map/while/body/eval_jaxpr/ppermute | solution.py:23
  334.3 5.7 collective-permute-start.9
  343.6 6.9 collective-permute-done.5
  352.5 10.1 %collective-permute-start.7 = (f32[16,2,1,256]{3,2,0,1:T(1,128)S(1)}, f32[16,2,1,256]{3,2,0,1:T(1,128)S(1)}, u32[]{:S(2)}, u32[]{:S(2)}) collective-permute-start(f32[16,2,1,256]{3,2,0,1:T(1,128)S(1)} %get-tuple-element.730), channel_id=1, source_target_pairs={{0,1},{1,2},{2,3},{3,4},{4,5},{5,6},{6,7},{7,8},{8,9},{9,10},{10,1... | collective-permute-start | bytes 98312 | tf_op jit(solution)/shard_map/while/body/eval_jaxpr/ppermute | solution.py:23
  366.5 5.7 collective-permute-start.9
  375.9 6.6 collective-permute-done.5
  384.5 10.1 %collective-permute-start.7 = (f32[16,2,1,256]{3,2,0,1:T(1,128)S(1)}, f32[16,2,1,256]{3,2,0,1:T(1,128)S(1)}, u32[]{:S(2)}, u32[]{:S(2)}) collective-permute-start(f32[16,2,1,256]{3,2,0,1:T(1,128)S(1)} %get-tuple-element.730), channel_id=1, source_target_pairs={{0,1},{1,2},{2,3},{3,4},{4,5},{5,6},{6,7},{7,8},{8,9},{9,10},{10,1... | collective-permute-start | bytes 98312 | tf_op jit(solution)/shard_map/while/body/eval_jaxpr/ppermute | solution.py:23
  398.5 5.7 collective-permute-start.9
  407.9 6.6 collective-permute-done.5
  416.5 10.1 %collective-permute-start.7 = (f32[16,2,1,256]{3,2,0,1:T(1,128)S(1)}, f32[16,2,1,256]{3,2,0,1:T(1,128)S(1)}, u32[]{:S(2)}, u32[]{:S(2)}) collective-permute-start(f32[16,2,1,256]{3,2,0,1:T(1,128)S(1)} %get-tuple-element.730), channel_id=1, source_target_pairs={{0,1},{1,2},{2,3},{3,4},{4,5},{5,6},{6,7},{7,8},{8,9},{9,10},{10,1... | collective-permute-start | bytes 98312 | tf_op jit(solution)/shard_map/while/body/eval_jaxpr/ppermute | solution.py:23
  430.5 5.7 collective-permute-start.9
  439.9 6.6 collective-permute-done.5
  448.5 10.1 %collective-permute-start.7 = (f32[16,2,1,256]{3,2,0,1:T(1,128)S(1)}, f32[16,2,1,256]{3,2,0,1:T(1,128)S(1)}, u32[]{:S(2)}, u32[]{:S(2)}) collective-permute-start(f32[16,2,1,256]{3,2,0,1:T(1,128)S(1)} %get-tuple-element.730), channel_id=1, source_target_pairs={{0,1},{1,2},{2,3},{3,4},{4,5},{5,6},{6,7},{7,8},{8,9},{9,10},{10,1... | collective-permute-start | bytes 98312 | tf_op jit(solution)/shard_map/while/body/eval_jaxpr/ppermute | solution.py:23
  462.5 5.7 collective-permute-start.9
  471.9 6.6 collective-permute-done.5
  480.5 10.1 %collective-permute-start.7 = (f32[16,2,1,256]{3,2,0,1:T(1,128)S(1)}, f32[16,2,1,256]{3,2,0,1:T(1,128)S(1)}, u32[]{:S(2)}, u32[]{:S(2)}) collective-permute-start(f32[16,2,1,256]{3,2,0,1:T(1,128)S(1)} %get-tuple-element.730), channel_id=1, source_target_pairs={{0,1},{1,2},{2,3},{3,4},{4,5},{5,6},{6,7},{7,8},{8,9},{9,10},{10,1... | collective-permute-start | bytes 98312 | tf_op jit(solution)/shard_map/while/body/eval_jaxpr/ppermute | solution.py:23
  494.5 5.7 collective-permute-start.9
  503.9 6.6 collective-permute-done.5
  512.5 10.1 %collective-permute-start.7 = (f32[16,2,1,256]{3,2,0,1:T(1,128)S(1)}, f32[16,2,1,256]{3,2,0,1:T(1,128)S(1)}, u32[]{:S(2)}, u32[]{:S(2)}) collective-permute-start(f32[16,2,1,256]{3,2,0,1:T(1,128)S(1)} %get-tuple-element.730), channel_id=1, source_target_pairs={{0,1},{1,2},{2,3},{3,4},{4,5},{5,6},{6,7},{7,8},{8,9},{9,10},{10,1... | collective-permute-start | bytes 98312 | tf_op jit(solution)/shard_map/while/body/eval_jaxpr/ppermute | solution.py:23
  526.6 5.7 collective-permute-start.9
  535.9 6.6 collective-permute-done.5
  544.5 10.1 %collective-permute-start.7 = (f32[16,2,1,256]{3,2,0,1:T(1,128)S(1)}, f32[16,2,1,256]{3,2,0,1:T(1,128)S(1)}, u32[]{:S(2)}, u32[]{:S(2)}) collective-permute-start(f32[16,2,1,256]{3,2,0,1:T(1,128)S(1)} %get-tuple-element.730), channel_id=1, source_target_pairs={{0,1},{1,2},{2,3},{3,4},{4,5},{5,6},{6,7},{7,8},{8,9},{9,10},{10,1... | collective-permute-start | bytes 98312 | tf_op jit(solution)/shard_map/while/body/eval_jaxpr/ppermute | solution.py:23
  558.6 5.7 collective-permute-start.9
  566.6 4.3 collective-permute-start.16
  574.7 5.8 collective-permute-done.17
  580.7 10.6 %collective-permute-start.18 = (f32[16,2,4,1,256]{4,3,2,0,1:T(1,128)S(1)}, f32[16,2,4,1,256]{4,3,2,0,1:T(1,128)S(1)}, u32[]{:S(2)}, u32[]{:S(2)}) collective-permute-start(f32[16,2,4,1,256]{4,3,2,0,1:T(1,128)S(1)} %get-tuple-element.567), channel_id=1, source_target_pairs={{0,1},{1,2},{2,3},{3,4},{4,5},{5,6},{6,7},{7,8},{8,9},{9,10},{10,1... | collective-permute-start | bytes 393224 | tf_op jit(solution)/shard_map/ppermute | solution.py:23
  593.4 8.1 fusion.50
  609.6 274.7 %all-reduce.13.cloned.1.call-done = f32[16,1027]{1,0:T(8,128)} async-done(((f32[16,1027]{1,0:T(8,128)}), f32[16,1027]{1,0:T(8,128)}) %all-reduce.13.cloned.1.call-update) | async-done | bytes 65744 | tf_op jit(solution)/shard_map/psum | solution.py:257
  (451 shorter events, 200.6 us)
Async XLA Ops:
  7.2 877.1 %all-reduce.13.cloned.1.call-start = ((), (), s32[]{:S(2)}) async-start(), calls=%async_computation | async-start | bytes 147456 | tf_op jit(solution)/shard_map/psum | solution.py:257
  8.4 23.0 %collective-permute-start.10 = (f32[16,2,1,8,256]{4,3,2,0,1:T(8,128)S(1)}, f32[16,2,1,8,256]{4,3,2,0,1:T(8,128)S(1)}, u32[]{:S(2)}, u32[]{:S(2)}) collective-permute-start(f32[16,2,1,8,256]{4,3,2,0,1:T(8,128)S(1)} %get-tuple-element.576), channel_id=1, source_target_pairs={{0,32},{32,64},{64,96},{96,128},{128,160},{160,192},{192,224},{1,3... | collective-permute-start | bytes 786440 | tf_op jit(solution)/shard_map/ppermute | solution.py:23
  12.3 19.1 %collective-permute-start.11 = (f32[16,2,1,8,256]{4,3,2,0,1:T(8,128)S(1)}, f32[16,2,1,8,256]{4,3,2,0,1:T(8,128)S(1)}, u32[]{:S(2)}, u32[]{:S(2)}) collective-permute-start(f32[16,2,1,8,256]{4,3,2,0,1:T(8,128)S(1)} %get-tuple-element.575), channel_id=1, source_target_pairs={{32,0},{64,32},{96,64},{128,96},{160,128},{192,160},{224,192},{33,... | collective-permute-start | bytes 786440 | tf_op jit(solution)/shard_map/ppermute | solution.py:24
  14.4 31.6 %collective-permute-start.14 = (f32[2,1,256]{2,1,0:T(1,128)S(1)}, f32[2,1,256]{2,1,0:T(1,128)S(1)}, u32[]{:S(2)}, u32[]{:S(2)}) collective-permute-start(f32[2,1,256]{2,1,0:T(1,128)S(1)} %get-tuple-element.587), channel_id=1, source_target_pairs={{0,1},{1,2},{2,3},{3,4},{4,5},{5,6},{6,7},{7,8},{8,9},{9,10},{10,1... | collective-permute-start | bytes 6152 | tf_op jit(solution)/shard_map/ppermute | solution.py:23
  19.6 28.4 %collective-permute-start.15 = (f32[2,1,256]{2,1,0:T(1,128)S(1)}, f32[2,1,256]{2,1,0:T(1,128)S(1)}, u32[]{:S(2)}, u32[]{:S(2)}) collective-permute-start(f32[2,1,256]{2,1,0:T(1,128)S(1)} %get-tuple-element.588), channel_id=1, source_target_pairs={{1,0},{2,1},{3,2},{4,3},{5,4},{6,5},{7,6},{8,7},{9,8},{10,9},{11,1... | collective-permute-start | bytes 6152 | tf_op jit(solution)/shard_map/ppermute | solution.py:24
  32.3 15.7 %collective-permute-start.12 = (f32[16,2,4,1,256]{4,3,2,0,1:T(1,128)}, f32[16,2,4,1,256]{4,3,2,0,1:T(1,128)}, u32[]{:S(2)}, u32[]{:S(2)}) collective-permute-start(f32[16,2,4,1,256]{4,3,2,0,1:T(1,128)} %get-tuple-element.569), channel_id=1, source_target_pairs={{0,1},{1,2},{2,3},{3,4},{4,5},{5,6},{6,7},{7,8},{8,9},{9,10},{10,1... | collective-permute-start | bytes 393224 | tf_op jit(solution)/shard_map/ppermute | solution.py:23
  37.5 10.6 %collective-permute-start.13 = (f32[16,2,4,1,256]{4,3,2,0,1:T(1,128)}, f32[16,2,4,1,256]{4,3,2,0,1:T(1,128)}, u32[]{:S(2)}, u32[]{:S(2)}) collective-permute-start(f32[16,2,4,1,256]{4,3,2,0,1:T(1,128)} %get-tuple-element.570), channel_id=1, source_target_pairs={{1,0},{2,1},{3,2},{4,3},{5,4},{6,5},{7,6},{8,7},{9,8},{10,9},{11,1... | collective-permute-start | bytes 393224 | tf_op jit(solution)/shard_map/ppermute | solution.py:24
  40.9 530.1 %collective-permute-start.20 = (f32[16,2,2,1,256]{4,3,2,0,1:T(1,128)}, f32[16,2,2,1,256]{4,3,2,0,1:T(1,128)}, u32[]{:S(2)}, u32[]{:S(2)}) collective-permute-start(f32[16,2,2,1,256]{4,3,2,0,1:T(1,128)} %get-tuple-element.571), channel_id=1, source_target_pairs={{0,1},{1,2},{2,3},{3,4},{4,5},{5,6},{6,7},{7,8},{8,9},{9,10},{10,1... | collective-permute-start | bytes 196616 | tf_op jit(solution)/shard_map/ppermute | solution.py:23
  46.1 525.0 %collective-permute-start.21 = (f32[16,2,2,1,256]{4,3,2,0,1:T(1,128)}, f32[16,2,2,1,256]{4,3,2,0,1:T(1,128)}, u32[]{:S(2)}, u32[]{:S(2)}) collective-permute-start(f32[16,2,2,1,256]{4,3,2,0,1:T(1,128)} %get-tuple-element.572), channel_id=1, source_target_pairs={{1,0},{2,1},{3,2},{4,3},{5,4},{6,5},{7,6},{8,7},{9,8},{10,9},{11,1... | collective-permute-start | bytes 196616 | tf_op jit(solution)/shard_map/ppermute | solution.py:24
  62.2 10.4 %collective-permute-start.1 = (f32[16,2,1,256]{3,2,1,0:T(1,128)S(1)}, f32[16,2,1,256]{3,2,1,0:T(1,128)S(1)}, u32[]{:S(2)}, u32[]{:S(2)}) collective-permute-start(f32[16,2,1,256]{3,2,1,0:T(1,128)S(1)} %get-tuple-element.706), channel_id=1, source_target_pairs={{1,0},{2,1},{3,2},{4,3},{5,4},{6,5},{7,6},{8,7},{9,8},{10,9},{11,1... | collective-permute-start | bytes 98312 | tf_op jit(solution)/shard_map/while/body/eval_jaxpr/ppermute | solution.py:24
  64.1 9.5 %collective-permute-start.2 = (f32[16,2,1,256]{3,2,1,0:T(1,128)S(1)}, f32[16,2,1,256]{3,2,1,0:T(1,128)S(1)}, u32[]{:S(2)}, u32[]{:S(2)}) collective-permute-start(f32[16,2,1,256]{3,2,1,0:T(1,128)S(1)} %get-tuple-element.707), channel_id=1, source_target_pairs={{0,1},{1,2},{2,3},{3,4},{4,5},{5,6},{6,7},{7,8},{8,9},{9,10},{10,1... | collective-permute-start | bytes 98312 | tf_op jit(solution)/shard_map/while/body/eval_jaxpr/ppermute | solution.py:23
  75.2 7.7 collective-permute-start.3
  92.2 11.7 %collective-permute-start.1 = (f32[16,2,1,256]{3,2,1,0:T(1,128)S(1)}, f32[16,2,1,256]{3,2,1,0:T(1,128)S(1)}, u32[]{:S(2)}, u32[]{:S(2)}) collective-permute-start(f32[16,2,1,256]{3,2,1,0:T(1,128)S(1)} %get-tuple-element.706), channel_id=1, source_target_pairs={{1,0},{2,1},{3,2},{4,3},{5,4},{6,5},{7,6},{8,7},{9,8},{10,9},{11,1... | collective-permute-start | bytes 98312 | tf_op jit(solution)/shard_map/while/body/eval_jaxpr/ppermute | solution.py:24
  94.1 10.8 %collective-permute-start.2 = (f32[16,2,1,256]{3,2,1,0:T(1,128)S(1)}, f32[16,2,1,256]{3,2,1,0:T(1,128)S(1)}, u32[]{:S(2)}, u32[]{:S(2)}) collective-permute-start(f32[16,2,1,256]{3,2,1,0:T(1,128)S(1)} %get-tuple-element.707), channel_id=1, source_target_pairs={{0,1},{1,2},{2,3},{3,4},{4,5},{5,6},{6,7},{7,8},{8,9},{9,10},{10,1... | collective-permute-start | bytes 98312 | tf_op jit(solution)/shard_map/while/body/eval_jaxpr/ppermute | solution.py:23
  116.4 8.1 collective-permute-start
  124.5 11.8 %collective-permute-start.1 = (f32[16,2,1,256]{3,2,1,0:T(1,128)S(1)}, f32[16,2,1,256]{3,2,1,0:T(1,128)S(1)}, u32[]{:S(2)}, u32[]{:S(2)}) collective-permute-start(f32[16,2,1,256]{3,2,1,0:T(1,128)S(1)} %get-tuple-element.706), channel_id=1, source_target_pairs={{1,0},{2,1},{3,2},{4,3},{5,4},{6,5},{7,6},{8,7},{9,8},{10,9},{11,1... | collective-permute-start | bytes 98312 | tf_op jit(solution)/shard_map/while/body/eval_jaxpr/ppermute | solution.py:24
  126.5 10.8 %collective-permute-start.2 = (f32[16,2,1,256]{3,2,1,0:T(1,128)S(1)}, f32[16,2,1,256]{3,2,1,0:T(1,128)S(1)}, u32[]{:S(2)}, u32[]{:S(2)}) collective-permute-start(f32[16,2,1,256]{3,2,1,0:T(1,128)S(1)} %get-tuple-element.707), channel_id=1, source_target_pairs={{0,1},{1,2},{2,3},{3,4},{4,5},{5,6},{6,7},{7,8},{8,9},{9,10},{10,1... | collective-permute-start | bytes 98312 | tf_op jit(solution)/shard_map/while/body/eval_jaxpr/ppermute | solution.py:23
  149.0 7.7 collective-permute-start
  156.7 11.8 %collective-permute-start.1 = (f32[16,2,1,256]{3,2,1,0:T(1,128)S(1)}, f32[16,2,1,256]{3,2,1,0:T(1,128)S(1)}, u32[]{:S(2)}, u32[]{:S(2)}) collective-permute-start(f32[16,2,1,256]{3,2,1,0:T(1,128)S(1)} %get-tuple-element.706), channel_id=1, source_target_pairs={{1,0},{2,1},{3,2},{4,3},{5,4},{6,5},{7,6},{8,7},{9,8},{10,9},{11,1... | collective-permute-start | bytes 98312 | tf_op jit(solution)/shard_map/while/body/eval_jaxpr/ppermute | solution.py:24
  158.6 10.8 %collective-permute-start.2 = (f32[16,2,1,256]{3,2,1,0:T(1,128)S(1)}, f32[16,2,1,256]{3,2,1,0:T(1,128)S(1)}, u32[]{:S(2)}, u32[]{:S(2)}) collective-permute-start(f32[16,2,1,256]{3,2,1,0:T(1,128)S(1)} %get-tuple-element.707), channel_id=1, source_target_pairs={{0,1},{1,2},{2,3},{3,4},{4,5},{5,6},{6,7},{7,8},{8,9},{9,10},{10,1... | collective-permute-start | bytes 98312 | tf_op jit(solution)/shard_map/while/body/eval_jaxpr/ppermute | solution.py:23
  181.2 7.7 collective-permute-start
  188.9 11.8 %collective-permute-start.1 = (f32[16,2,1,256]{3,2,1,0:T(1,128)S(1)}, f32[16,2,1,256]{3,2,1,0:T(1,128)S(1)}, u32[]{:S(2)}, u32[]{:S(2)}) collective-permute-start(f32[16,2,1,256]{3,2,1,0:T(1,128)S(1)} %get-tuple-element.706), channel_id=1, source_target_pairs={{1,0},{2,1},{3,2},{4,3},{5,4},{6,5},{7,6},{8,7},{9,8},{10,9},{11,1... | collective-permute-start | bytes 98312 | tf_op jit(solution)/shard_map/while/body/eval_jaxpr/ppermute | solution.py:24
  190.8 10.8 %collective-permute-start.2 = (f32[16,2,1,256]{3,2,1,0:T(1,128)S(1)}, f32[16,2,1,256]{3,2,1,0:T(1,128)S(1)}, u32[]{:S(2)}, u32[]{:S(2)}) collective-permute-start(f32[16,2,1,256]{3,2,1,0:T(1,128)S(1)} %get-tuple-element.707), channel_id=1, source_target_pairs={{0,1},{1,2},{2,3},{3,4},{4,5},{5,6},{6,7},{7,8},{8,9},{9,10},{10,1... | collective-permute-start | bytes 98312 | tf_op jit(solution)/shard_map/while/body/eval_jaxpr/ppermute | solution.py:23
  213.4 7.7 collective-permute-start
  221.1 11.8 %collective-permute-start.1 = (f32[16,2,1,256]{3,2,1,0:T(1,128)S(1)}, f32[16,2,1,256]{3,2,1,0:T(1,128)S(1)}, u32[]{:S(2)}, u32[]{:S(2)}) collective-permute-start(f32[16,2,1,256]{3,2,1,0:T(1,128)S(1)} %get-tuple-element.706), channel_id=1, source_target_pairs={{1,0},{2,1},{3,2},{4,3},{5,4},{6,5},{7,6},{8,7},{9,8},{10,9},{11,1... | collective-permute-start | bytes 98312 | tf_op jit(solution)/shard_map/while/body/eval_jaxpr/ppermute | solution.py:24
  223.0 10.8 %collective-permute-start.2 = (f32[16,2,1,256]{3,2,1,0:T(1,128)S(1)}, f32[16,2,1,256]{3,2,1,0:T(1,128)S(1)}, u32[]{:S(2)}, u32[]{:S(2)}) collective-permute-start(f32[16,2,1,256]{3,2,1,0:T(1,128)S(1)} %get-tuple-element.707), channel_id=1, source_target_pairs={{0,1},{1,2},{2,3},{3,4},{4,5},{5,6},{6,7},{7,8},{8,9},{9,10},{10,1... | collective-permute-start | bytes 98312 | tf_op jit(solution)/shard_map/while/body/eval_jaxpr/ppermute | solution.py:23
  245.6 7.7 collective-permute-start
  253.3 11.8 %collective-permute-start.1 = (f32[16,2,1,256]{3,2,1,0:T(1,128)S(1)}, f32[16,2,1,256]{3,2,1,0:T(1,128)S(1)}, u32[]{:S(2)}, u32[]{:S(2)}) collective-permute-start(f32[16,2,1,256]{3,2,1,0:T(1,128)S(1)} %get-tuple-element.706), channel_id=1, source_target_pairs={{1,0},{2,1},{3,2},{4,3},{5,4},{6,5},{7,6},{8,7},{9,8},{10,9},{11,1... | collective-permute-start | bytes 98312 | tf_op jit(solution)/shard_map/while/body/eval_jaxpr/ppermute | solution.py:24
  255.3 10.8 %collective-permute-start.2 = (f32[16,2,1,256]{3,2,1,0:T(1,128)S(1)}, f32[16,2,1,256]{3,2,1,0:T(1,128)S(1)}, u32[]{:S(2)}, u32[]{:S(2)}) collective-permute-start(f32[16,2,1,256]{3,2,1,0:T(1,128)S(1)} %get-tuple-element.707), channel_id=1, source_target_pairs={{0,1},{1,2},{2,3},{3,4},{4,5},{5,6},{6,7},{7,8},{8,9},{9,10},{10,1... | collective-permute-start | bytes 98312 | tf_op jit(solution)/shard_map/while/body/eval_jaxpr/ppermute | solution.py:23
  277.8 7.7 collective-permute-start
  285.5 11.8 %collective-permute-start.1 = (f32[16,2,1,256]{3,2,1,0:T(1,128)S(1)}, f32[16,2,1,256]{3,2,1,0:T(1,128)S(1)}, u32[]{:S(2)}, u32[]{:S(2)}) collective-permute-start(f32[16,2,1,256]{3,2,1,0:T(1,128)S(1)} %get-tuple-element.706), channel_id=1, source_target_pairs={{1,0},{2,1},{3,2},{4,3},{5,4},{6,5},{7,6},{8,7},{9,8},{10,9},{11,1... | collective-permute-start | bytes 98312 | tf_op jit(solution)/shard_map/while/body/eval_jaxpr/ppermute | solution.py:24
  287.5 10.8 %collective-permute-start.2 = (f32[16,2,1,256]{3,2,1,0:T(1,128)S(1)}, f32[16,2,1,256]{3,2,1,0:T(1,128)S(1)}, u32[]{:S(2)}, u32[]{:S(2)}) collective-permute-start(f32[16,2,1,256]{3,2,1,0:T(1,128)S(1)} %get-tuple-element.707), channel_id=1, source_target_pairs={{0,1},{1,2},{2,3},{3,4},{4,5},{5,6},{6,7},{7,8},{8,9},{9,10},{10,1... | collective-permute-start | bytes 98312 | tf_op jit(solution)/shard_map/while/body/eval_jaxpr/ppermute | solution.py:23
  309.9 8.2 collective-permute-start.5
  318.1 12.3 %collective-permute-start.6 = (f32[16,2,1,256]{3,2,0,1:T(1,128)S(1)}, f32[16,2,1,256]{3,2,0,1:T(1,128)S(1)}, u32[]{:S(2)}, u32[]{:S(2)}) collective-permute-start(f32[16,2,1,256]{3,2,0,1:T(1,128)S(1)} %get-tuple-element.729), channel_id=1, source_target_pairs={{1,0},{2,1},{3,2},{4,3},{5,4},{6,5},{7,6},{8,7},{9,8},{10,9},{11,1... | collective-permute-start | bytes 98312 | tf_op jit(solution)/shard_map/while/body/eval_jaxpr/ppermute | solution.py:24
  320.0 11.3 %collective-permute-start.7 = (f32[16,2,1,256]{3,2,0,1:T(1,128)S(1)}, f32[16,2,1,256]{3,2,0,1:T(1,128)S(1)}, u32[]{:S(2)}, u32[]{:S(2)}) collective-permute-start(f32[16,2,1,256]{3,2,0,1:T(1,128)S(1)} %get-tuple-element.730), channel_id=1, source_target_pairs={{0,1},{1,2},{2,3},{3,4},{4,5},{5,6},{6,7},{7,8},{8,9},{9,10},{10,1... | collective-permute-start | bytes 98312 | tf_op jit(solution)/shard_map/while/body/eval_jaxpr/ppermute | solution.py:23
  332.4 7.7 collective-permute-start.8
  342.3 8.2 collective-permute-start.5
  350.5 12.1 %collective-permute-start.6 = (f32[16,2,1,256]{3,2,0,1:T(1,128)S(1)}, f32[16,2,1,256]{3,2,0,1:T(1,128)S(1)}, u32[]{:S(2)}, u32[]{:S(2)}) collective-permute-start(f32[16,2,1,256]{3,2,0,1:T(1,128)S(1)} %get-tuple-element.729), channel_id=1, source_target_pairs={{1,0},{2,1},{3,2},{4,3},{5,4},{6,5},{7,6},{8,7},{9,8},{10,9},{11,1... | collective-permute-start | bytes 98312 | tf_op jit(solution)/shard_map/while/body/eval_jaxpr/ppermute | solution.py:24
  352.5 11.1 %collective-permute-start.7 = (f32[16,2,1,256]{3,2,0,1:T(1,128)S(1)}, f32[16,2,1,256]{3,2,0,1:T(1,128)S(1)}, u32[]{:S(2)}, u32[]{:S(2)}) collective-permute-start(f32[16,2,1,256]{3,2,0,1:T(1,128)S(1)} %get-tuple-element.730), channel_id=1, source_target_pairs={{0,1},{1,2},{2,3},{3,4},{4,5},{5,6},{6,7},{7,8},{8,9},{9,10},{10,1... | collective-permute-start | bytes 98312 | tf_op jit(solution)/shard_map/while/body/eval_jaxpr/ppermute | solution.py:23
  364.6 7.7 collective-permute-start.8
  374.6 7.9 collective-permute-start.5
  382.5 12.1 %collective-permute-start.6 = (f32[16,2,1,256]{3,2,0,1:T(1,128)S(1)}, f32[16,2,1,256]{3,2,0,1:T(1,128)S(1)}, u32[]{:S(2)}, u32[]{:S(2)}) collective-permute-start(f32[16,2,1,256]{3,2,0,1:T(1,128)S(1)} %get-tuple-element.729), channel_id=1, source_target_pairs={{1,0},{2,1},{3,2},{4,3},{5,4},{6,5},{7,6},{8,7},{9,8},{10,9},{11,1... | collective-permute-start | bytes 98312 | tf_op jit(solution)/shard_map/while/body/eval_jaxpr/ppermute | solution.py:24
  384.5 11.1 %collective-permute-start.7 = (f32[16,2,1,256]{3,2,0,1:T(1,128)S(1)}, f32[16,2,1,256]{3,2,0,1:T(1,128)S(1)}, u32[]{:S(2)}, u32[]{:S(2)}) collective-permute-start(f32[16,2,1,256]{3,2,0,1:T(1,128)S(1)} %get-tuple-element.730), channel_id=1, source_target_pairs={{0,1},{1,2},{2,3},{3,4},{4,5},{5,6},{6,7},{7,8},{8,9},{9,10},{10,1... | collective-permute-start | bytes 98312 | tf_op jit(solution)/shard_map/while/body/eval_jaxpr/ppermute | solution.py:23
  396.6 7.7 collective-permute-start.8
  406.6 7.9 collective-permute-start.5
  414.5 12.1 %collective-permute-start.6 = (f32[16,2,1,256]{3,2,0,1:T(1,128)S(1)}, f32[16,2,1,256]{3,2,0,1:T(1,128)S(1)}, u32[]{:S(2)}, u32[]{:S(2)}) collective-permute-start(f32[16,2,1,256]{3,2,0,1:T(1,128)S(1)} %get-tuple-element.729), channel_id=1, source_target_pairs={{1,0},{2,1},{3,2},{4,3},{5,4},{6,5},{7,6},{8,7},{9,8},{10,9},{11,1... | collective-permute-start | bytes 98312 | tf_op jit(solution)/shard_map/while/body/eval_jaxpr/ppermute | solution.py:24
  416.5 11.1 %collective-permute-start.7 = (f32[16,2,1,256]{3,2,0,1:T(1,128)S(1)}, f32[16,2,1,256]{3,2,0,1:T(1,128)S(1)}, u32[]{:S(2)}, u32[]{:S(2)}) collective-permute-start(f32[16,2,1,256]{3,2,0,1:T(1,128)S(1)} %get-tuple-element.730), channel_id=1, source_target_pairs={{0,1},{1,2},{2,3},{3,4},{4,5},{5,6},{6,7},{7,8},{8,9},{9,10},{10,1... | collective-permute-start | bytes 98312 | tf_op jit(solution)/shard_map/while/body/eval_jaxpr/ppermute | solution.py:23
  428.6 7.7 collective-permute-start.8
  438.6 7.9 collective-permute-start.5
  446.5 12.1 %collective-permute-start.6 = (f32[16,2,1,256]{3,2,0,1:T(1,128)S(1)}, f32[16,2,1,256]{3,2,0,1:T(1,128)S(1)}, u32[]{:S(2)}, u32[]{:S(2)}) collective-permute-start(f32[16,2,1,256]{3,2,0,1:T(1,128)S(1)} %get-tuple-element.729), channel_id=1, source_target_pairs={{1,0},{2,1},{3,2},{4,3},{5,4},{6,5},{7,6},{8,7},{9,8},{10,9},{11,1... | collective-permute-start | bytes 98312 | tf_op jit(solution)/shard_map/while/body/eval_jaxpr/ppermute | solution.py:24
  448.5 11.1 %collective-permute-start.7 = (f32[16,2,1,256]{3,2,0,1:T(1,128)S(1)}, f32[16,2,1,256]{3,2,0,1:T(1,128)S(1)}, u32[]{:S(2)}, u32[]{:S(2)}) collective-permute-start(f32[16,2,1,256]{3,2,0,1:T(1,128)S(1)} %get-tuple-element.730), channel_id=1, source_target_pairs={{0,1},{1,2},{2,3},{3,4},{4,5},{5,6},{6,7},{7,8},{8,9},{9,10},{10,1... | collective-permute-start | bytes 98312 | tf_op jit(solution)/shard_map/while/body/eval_jaxpr/ppermute | solution.py:23
  460.6 7.7 collective-permute-start.8
  470.6 7.9 collective-permute-start.5
  478.5 12.1 %collective-permute-start.6 = (f32[16,2,1,256]{3,2,0,1:T(1,128)S(1)}, f32[16,2,1,256]{3,2,0,1:T(1,128)S(1)}, u32[]{:S(2)}, u32[]{:S(2)}) collective-permute-start(f32[16,2,1,256]{3,2,0,1:T(1,128)S(1)} %get-tuple-element.729), channel_id=1, source_target_pairs={{1,0},{2,1},{3,2},{4,3},{5,4},{6,5},{7,6},{8,7},{9,8},{10,9},{11,1... | collective-permute-start | bytes 98312 | tf_op jit(solution)/shard_map/while/body/eval_jaxpr/ppermute | solution.py:24
  480.5 11.1 %collective-permute-start.7 = (f32[16,2,1,256]{3,2,0,1:T(1,128)S(1)}, f32[16,2,1,256]{3,2,0,1:T(1,128)S(1)}, u32[]{:S(2)}, u32[]{:S(2)}) collective-permute-start(f32[16,2,1,256]{3,2,0,1:T(1,128)S(1)} %get-tuple-element.730), channel_id=1, source_target_pairs={{0,1},{1,2},{2,3},{3,4},{4,5},{5,6},{6,7},{7,8},{8,9},{9,10},{10,1... | collective-permute-start | bytes 98312 | tf_op jit(solution)/shard_map/while/body/eval_jaxpr/ppermute | solution.py:23
  502.6 7.9 collective-permute-start.5
  510.6 12.0 %collective-permute-start.6 = (f32[16,2,1,256]{3,2,0,1:T(1,128)S(1)}, f32[16,2,1,256]{3,2,0,1:T(1,128)S(1)}, u32[]{:S(2)}, u32[]{:S(2)}) collective-permute-start(f32[16,2,1,256]{3,2,0,1:T(1,128)S(1)} %get-tuple-element.729), channel_id=1, source_target_pairs={{1,0},{2,1},{3,2},{4,3},{5,4},{6,5},{7,6},{8,7},{9,8},{10,9},{11,1... | collective-permute-start | bytes 98312 | tf_op jit(solution)/shard_map/while/body/eval_jaxpr/ppermute | solution.py:24
  512.5 11.1 %collective-permute-start.7 = (f32[16,2,1,256]{3,2,0,1:T(1,128)S(1)}, f32[16,2,1,256]{3,2,0,1:T(1,128)S(1)}, u32[]{:S(2)}, u32[]{:S(2)}) collective-permute-start(f32[16,2,1,256]{3,2,0,1:T(1,128)S(1)} %get-tuple-element.730), channel_id=1, source_target_pairs={{0,1},{1,2},{2,3},{3,4},{4,5},{5,6},{6,7},{7,8},{8,9},{9,10},{10,1... | collective-permute-start | bytes 98312 | tf_op jit(solution)/shard_map/while/body/eval_jaxpr/ppermute | solution.py:23
  534.6 7.9 collective-permute-start.5
  542.6 12.0 %collective-permute-start.6 = (f32[16,2,1,256]{3,2,0,1:T(1,128)S(1)}, f32[16,2,1,256]{3,2,0,1:T(1,128)S(1)}, u32[]{:S(2)}, u32[]{:S(2)}) collective-permute-start(f32[16,2,1,256]{3,2,0,1:T(1,128)S(1)} %get-tuple-element.729), channel_id=1, source_target_pairs={{1,0},{2,1},{3,2},{4,3},{5,4},{6,5},{7,6},{8,7},{9,8},{10,9},{11,1... | collective-permute-start | bytes 98312 | tf_op jit(solution)/shard_map/while/body/eval_jaxpr/ppermute | solution.py:24
  544.5 11.1 %collective-permute-start.7 = (f32[16,2,1,256]{3,2,0,1:T(1,128)S(1)}, f32[16,2,1,256]{3,2,0,1:T(1,128)S(1)}, u32[]{:S(2)}, u32[]{:S(2)}) collective-permute-start(f32[16,2,1,256]{3,2,0,1:T(1,128)S(1)} %get-tuple-element.730), channel_id=1, source_target_pairs={{0,1},{1,2},{2,3},{3,4},{4,5},{5,6},{6,7},{7,8},{8,9},{9,10},{10,1... | collective-permute-start | bytes 98312 | tf_op jit(solution)/shard_map/while/body/eval_jaxpr/ppermute | solution.py:23
  566.6 8.0 collective-permute-start.16
  580.7 20.9 %collective-permute-start.18 = (f32[16,2,4,1,256]{4,3,2,0,1:T(1,128)S(1)}, f32[16,2,4,1,256]{4,3,2,0,1:T(1,128)S(1)}, u32[]{:S(2)}, u32[]{:S(2)}) collective-permute-start(f32[16,2,4,1,256]{4,3,2,0,1:T(1,128)S(1)} %get-tuple-element.567), channel_id=1, source_target_pairs={{0,1},{1,2},{2,3},{3,4},{4,5},{5,6},{6,7},{7,8},{8,9},{9,10},{10,1... | collective-permute-start | bytes 393224 | tf_op jit(solution)/shard_map/ppermute | solution.py:23
  591.3 10.4 %collective-permute-start.19 = (f32[16,2,4,1,256]{4,3,2,0,1:T(1,128)S(1)}, f32[16,2,4,1,256]{4,3,2,0,1:T(1,128)S(1)}, u32[]{:S(2)}, u32[]{:S(2)}) collective-permute-start(f32[16,2,4,1,256]{4,3,2,0,1:T(1,128)S(1)} %get-tuple-element.568), channel_id=1, source_target_pairs={{1,0},{2,1},{3,2},{4,3},{5,4},{6,5},{7,6},{8,7},{9,8},{10,9},{11,1... | collective-permute-start | bytes 393224 | tf_op jit(solution)/shard_map/ppermute | solution.py:24
  (46 other events, 381.7 us)
Sparse Core Ops, SparseCore 0:
  608.3 275.9 all-reduce.12
where the time goes:
time: 899 us; the launch traced here: 896 us
  starting transfers between devices  401 us (45%)
  waiting for transfers between devices  393 us (44%)
  other arithmetic  65.2 us (7%)
  between operations  14.7 us (2%)
  local copies, waits for them, and re-layouts  11.3 us (1%)
    ppermute x38, starting transfers between devices, extended(): before = lax.ppermute(last, axis, up)  284 us
    psum x1, waiting for transfers between devices, per_device(): packed = lax.psum(packed, ('depth', 'tile'))  275 us
    ppermute x16, waiting for transfers between devices, shifted(): lax.ppermute(value, axis, [(source, source + steps) for source in range(l...  80.2 us
    ppermute x38, starting transfers between devices, extended(): after = lax.ppermute(leading, axis, down)  71.8 us
    ppermute x16, starting transfers between devices, shifted(): lax.ppermute(value, axis, [(source, source + steps) for source in range(l...  44.6 us
    ppermute x38, waiting for transfers between devices, extended(): before = lax.ppermute(last, axis, up)  32.3 us
    concatenate x36, other arithmetic, extended(): shard = jnp.concatenate([before, shard, after], axis=dim)  20.3 us
  transfers between devices with their start and end apart: 93, of which 50 were waited for; matrix products, arithmetic and copies ran while one was open for 8% of the time, Pallas kernels for 0%

commit v1 on v0

--- a/solution.py
+++ b/solution.py
@@ -254,7 +254,7 @@
         [jnp.stack([local_real, local_imag, local_norm], axis=1), picked.reshape(shot_count, -1)],
         axis=1,
     )
-    packed = lax.psum(packed, ("depth", "tile"))
+    packed = jnp.sum(lax.all_gather(packed, ("depth", "tile")), axis=0)
     dot_real, dot_imag, image_norm = (packed[:, 0], packed[:, 1], packed[:, 2])
     picked = packed[:, 3:].reshape(shot_count, 4, -1)
     step_re = (dot_real / image_norm)[:, None, None, None]

time: 899 us -> 1080 us (1.20)
  waiting for transfers between devices: 393 us -> 589 us
  starting transfers between devices: 401 us -> 383 us
    all_gather x0 -> x1, waiting for transfers between devices: none -> 457 us  [per_device(): packed = jnp.sum(lax.all_gather(packed, ('depth', 'tile')), axis=0)]
    psum x1 -> x0, waiting for transfers between devices: 275 us -> none  [per_device(): packed = lax.psum(packed, ('depth', 'tile'))]
    ppermute x38, starting transfers between devices: 284 us -> 268 us  [extended(): before = lax.ppermute(last, axis, up)]
    ppermute x38, waiting for transfers between devices: 5.91 us -> 18.3 us  [extended(): after = lax.ppermute(leading, axis, down)]
  transfers between devices with their start and end apart: 93 -> 93, of which waited for: 50 -> 53; matrix products, arithmetic and copies ran while one was open for 8% -> 2% of each run, Pallas kernels for 0% -> 0%
where the time goes in v1:
time: 1080 us
  waiting for transfers between devices  589 us (55%)
  starting transfers between devices  383 us (35%)
  other arithmetic  68.4 us (6%)
  between operations  14.7 us (1%)
  local copies, waits for them, and re-layouts  10.8 us (1%)
    all_gather x1, waiting for transfers between devices, per_device(): packed = jnp.sum(lax.all_gather(packed, ('depth', 'tile')), axis=0)  457 us
    ppermute x38, starting transfers between devices, extended(): before = lax.ppermute(last, axis, up)  268 us
    ppermute x16, waiting for transfers between devices, shifted(): lax.ppermute(value, axis, [(source, source + steps) for source in range(l...  79.5 us
    ppermute x38, starting transfers between devices, extended(): after = lax.ppermute(leading, axis, down)  71.8 us
    ppermute x16, starting transfers between devices, shifted(): lax.ppermute(value, axis, [(source, source + steps) for source in range(l...  43.2 us
    ppermute x38, waiting for transfers between devices, extended(): before = lax.ppermute(last, axis, up)  34.2 us
  transfers between devices with their start and end apart: 93, of which 53 were waited for; matrix products, arithmetic and copies ran while one was open for 2% of the time, Pallas kernels for 0%

profile of v1, /device:TPU:1, one launch (start us, length us, event | category | flops | bytes accessed | tf_op | source)
XLA Modules:
  0.0 1076.4 jit_solution(9179622799882042308)
XLA Ops:
  8.4 3.9 collective-permute-start.10
  14.4 5.2 collective-permute-start.14
  28.8 5.1 collective-permute-start.12
  36.9 5.2 collective-permute-done.13
  44.7 3.6 fusion.119
  48.7 247.5 %while.36 = (s32[]{:T(128)}, f32[16,2,2,8,256]{4,3,2,1,0:T(8,128)S(1)}, f32[16,2,8,256]{3,2,1,0:T(8,128)S(1)}, s32[]{:T(128)}, f32[2,8,256]{2,1,0:T(8,128)S(1)},...) while((s32[]{:T(128)}, ...), condition=%wide.region_1.2_spmd.clone, body=%wide.region_0.1_spmd.clone.sunk | while | flops 5369095 | bytes 13800788 | solution.py:214
  48.7 3.7 collective-permute-start
  52.4 3.3 collective-permute-done
  57.7 5.1 collective-permute-start.2
  67.3 5.7 collective-permute-start.4
  75.3 5.0 collective-permute-start
  85.6 9.5 collective-permute-start.2
  99.6 5.9 collective-permute-start.4
  107.7 3.6 collective-permute-start
  116.5 9.3 collective-permute-start.2
  130.5 5.9 collective-permute-start.4
  138.6 4.1 collective-permute-start
  148.0 9.2 collective-permute-start.2
  162.0 5.9 collective-permute-start.4
  170.1 4.1 collective-permute-start
  179.6 9.2 collective-permute-start.2
  193.5 5.9 collective-permute-start.4
  201.7 4.1 collective-permute-start
  211.1 9.2 collective-permute-start.2
  225.0 5.9 collective-permute-start.4
  233.2 4.1 collective-permute-start
  242.6 9.2 collective-permute-start.2
  256.5 5.9 collective-permute-start.4
  264.7 4.1 collective-permute-start
  274.1 9.2 collective-permute-start.2
  288.1 5.9 collective-permute-start.4
  296.2 247.9 %while.37 = (s32[]{:T(128)}, f32[16,2,2,8,256]{4,3,2,1,0:T(8,128)S(1)}, f32[16,2,8,256]{3,2,0,1:T(8,128)S(1)}, s32[]{:T(128)}, f32[16,2,2,8,256]{4,3,0,1,2:T(8,1...) while((s32[]{:T(128)}, ...), condition=%wide.region_3.4_spmd.clone, body=%wide.region_2.3_spmd.clone.sunk | while | flops 5318663 | bytes 15177044 | solution.py:214
  297.6 6.6 collective-permute-done.5
  306.1 9.0 collective-permute-start.7
  319.3 5.9 collective-permute-start.9
  328.8 6.2 collective-permute-done.5
  337.0 7.7 collective-permute-start.7
  348.6 5.7 collective-permute-start.9
  358.0 6.7 collective-permute-done.5
  366.6 7.2 collective-permute-start.7
  377.8 5.7 collective-permute-start.9
  387.1 6.7 collective-permute-done.5
  395.8 9.4 collective-permute-start.7
  409.2 5.8 collective-permute-start.9
  418.6 6.8 collective-permute-done.5
  427.3 9.9 collective-permute-start.7
  441.2 5.8 collective-permute-start.9
  450.5 6.8 collective-permute-done.5
  459.3 9.9 collective-permute-start.7
  473.2 5.8 collective-permute-start.9
  482.5 6.8 collective-permute-done.5
  491.3 9.9 collective-permute-start.7
  505.1 5.8 collective-permute-start.9
  514.5 6.8 collective-permute-done.5
  523.3 8.9 collective-permute-start.7
  536.1 5.8 collective-permute-start.9
  544.2 3.9 collective-permute-start.16
  551.7 6.9 collective-permute-done.17
  558.8 9.7 collective-permute-start.18
  570.6 8.1 fusion.50
  586.7 5.1 collective-permute-start.20
  593.9 6.1 collective-permute-done.21
  601.4 456.6 %all-gather.3.cloned.1.call-done = f32[4096,1027]{1,0:T(8,128)} async-done(((f32[16,1027]{1,0:T(8,128)}), f32[4096,1027]{1,0:T(8,128)}) %all-gather.3.cloned.1.call-update) | async-done | bytes 16826384 | tf_op jit(solution)/shard_map/all_gather | solution.py:257
  1058.0 7.3 reduce_sum.67
  (460 shorter events, 207.7 us)
Async XLA Ops:
  7.2 1050.8 %all-gather.3.cloned.1.call-start = ((), (), s32[]{:S(2)}) async-start(), calls=%async_computation | async-start | bytes 18948096 | tf_op jit(solution)/shard_map/all_gather | solution.py:257
  8.4 19.5 %collective-permute-start.10 = (f32[16,2,1,8,256]{4,3,2,0,1:T(8,128)S(1)}, f32[16,2,1,8,256]{4,3,2,0,1:T(8,128)S(1)}, u32[]{:S(2)}, u32[]{:S(2)}) collective-permute-start(f32[16,2,1,8,256]{4,3,2,0,1:T(8,128)S(1)} %get-tuple-element.662), channel_id=1, source_target_pairs={{0,32},{32,64},{64,96},{96,128},{128,160},{160,192},{192,224},{1,3... | collective-permute-start | bytes 786440 | tf_op jit(solution)/shard_map/ppermute | solution.py:23
  12.3 15.6 %collective-permute-start.11 = (f32[16,2,1,8,256]{4,3,2,0,1:T(8,128)S(1)}, f32[16,2,1,8,256]{4,3,2,0,1:T(8,128)S(1)}, u32[]{:S(2)}, u32[]{:S(2)}) collective-permute-start(f32[16,2,1,8,256]{4,3,2,0,1:T(8,128)S(1)} %get-tuple-element.661), channel_id=1, source_target_pairs={{32,0},{64,32},{96,64},{128,96},{160,128},{192,160},{224,192},{33,... | collective-permute-start | bytes 786440 | tf_op jit(solution)/shard_map/ppermute | solution.py:24
  14.4 22.4 %collective-permute-start.14 = (f32[2,1,256]{2,1,0:T(1,128)S(1)}, f32[2,1,256]{2,1,0:T(1,128)S(1)}, u32[]{:S(2)}, u32[]{:S(2)}) collective-permute-start(f32[2,1,256]{2,1,0:T(1,128)S(1)} %get-tuple-element.672), channel_id=1, source_target_pairs={{0,1},{1,2},{2,3},{3,4},{4,5},{5,6},{6,7},{7,8},{8,9},{9,10},{10,1... | collective-permute-start | bytes 6152 | tf_op jit(solution)/shard_map/ppermute | solution.py:23
  19.6 17.2 %collective-permute-start.15 = (f32[2,1,256]{2,1,0:T(1,128)S(1)}, f32[2,1,256]{2,1,0:T(1,128)S(1)}, u32[]{:S(2)}, u32[]{:S(2)}) collective-permute-start(f32[2,1,256]{2,1,0:T(1,128)S(1)} %get-tuple-element.673), channel_id=1, source_target_pairs={{1,0},{2,1},{3,2},{4,3},{5,4},{6,5},{7,6},{8,7},{9,8},{10,9},{11,1... | collective-permute-start | bytes 6152 | tf_op jit(solution)/shard_map/ppermute | solution.py:24
  28.8 8.1 collective-permute-start.12
  34.0 8.1 collective-permute-start.13
  75.3 8.3 collective-permute-start
  83.6 11.4 %collective-permute-start.1 = (f32[16,2,1,256]{3,2,1,0:T(1,128)S(1)}, f32[16,2,1,256]{3,2,1,0:T(1,128)S(1)}, u32[]{:S(2)}, u32[]{:S(2)}) collective-permute-start(f32[16,2,1,256]{3,2,1,0:T(1,128)S(1)} %get-tuple-element.793), channel_id=1, source_target_pairs={{1,0},{2,1},{3,2},{4,3},{5,4},{6,5},{7,6},{8,7},{9,8},{10,9},{11,1... | collective-permute-start | bytes 98312 | tf_op jit(solution)/shard_map/while/body/eval_jaxpr/ppermute | solution.py:24
  85.6 10.5 collective-permute-start.2
  97.6 7.8 collective-permute-start.3
  114.6 11.2 %collective-permute-start.1 = (f32[16,2,1,256]{3,2,1,0:T(1,128)S(1)}, f32[16,2,1,256]{3,2,1,0:T(1,128)S(1)}, u32[]{:S(2)}, u32[]{:S(2)}) collective-permute-start(f32[16,2,1,256]{3,2,1,0:T(1,128)S(1)} %get-tuple-element.793), channel_id=1, source_target_pairs={{1,0},{2,1},{3,2},{4,3},{5,4},{6,5},{7,6},{8,7},{9,8},{10,9},{11,1... | collective-permute-start | bytes 98312 | tf_op jit(solution)/shard_map/while/body/eval_jaxpr/ppermute | solution.py:24
  116.5 10.4 collective-permute-start.2
  128.6 7.8 collective-permute-start.3
  146.1 11.2 %collective-permute-start.1 = (f32[16,2,1,256]{3,2,1,0:T(1,128)S(1)}, f32[16,2,1,256]{3,2,1,0:T(1,128)S(1)}, u32[]{:S(2)}, u32[]{:S(2)}) collective-permute-start(f32[16,2,1,256]{3,2,1,0:T(1,128)S(1)} %get-tuple-element.793), channel_id=1, source_target_pairs={{1,0},{2,1},{3,2},{4,3},{5,4},{6,5},{7,6},{8,7},{9,8},{10,9},{11,1... | collective-permute-start | bytes 98312 | tf_op jit(solution)/shard_map/while/body/eval_jaxpr/ppermute | solution.py:24
  148.0 10.4 collective-permute-start.2
  160.1 7.8 collective-permute-start.3
  177.6 11.2 %collective-permute-start.1 = (f32[16,2,1,256]{3,2,1,0:T(1,128)S(1)}, f32[16,2,1,256]{3,2,1,0:T(1,128)S(1)}, u32[]{:S(2)}, u32[]{:S(2)}) collective-permute-start(f32[16,2,1,256]{3,2,1,0:T(1,128)S(1)} %get-tuple-element.793), channel_id=1, source_target_pairs={{1,0},{2,1},{3,2},{4,3},{5,4},{6,5},{7,6},{8,7},{9,8},{10,9},{11,1... | collective-permute-start | bytes 98312 | tf_op jit(solution)/shard_map/while/body/eval_jaxpr/ppermute | solution.py:24
  179.6 10.4 collective-permute-start.2
  191.6 7.8 collective-permute-start.3
  209.1 11.2 %collective-permute-start.1 = (f32[16,2,1,256]{3,2,1,0:T(1,128)S(1)}, f32[16,2,1,256]{3,2,1,0:T(1,128)S(1)}, u32[]{:S(2)}, u32[]{:S(2)}) collective-permute-start(f32[16,2,1,256]{3,2,1,0:T(1,128)S(1)} %get-tuple-element.793), channel_id=1, source_target_pairs={{1,0},{2,1},{3,2},{4,3},{5,4},{6,5},{7,6},{8,7},{9,8},{10,9},{11,1... | collective-permute-start | bytes 98312 | tf_op jit(solution)/shard_map/while/body/eval_jaxpr/ppermute | solution.py:24
  211.1 10.4 collective-permute-start.2
  223.1 7.8 collective-permute-start.3
  240.7 11.2 %collective-permute-start.1 = (f32[16,2,1,256]{3,2,1,0:T(1,128)S(1)}, f32[16,2,1,256]{3,2,1,0:T(1,128)S(1)}, u32[]{:S(2)}, u32[]{:S(2)}) collective-permute-start(f32[16,2,1,256]{3,2,1,0:T(1,128)S(1)} %get-tuple-element.793), channel_id=1, source_target_pairs={{1,0},{2,1},{3,2},{4,3},{5,4},{6,5},{7,6},{8,7},{9,8},{10,9},{11,1... | collective-permute-start | bytes 98312 | tf_op jit(solution)/shard_map/while/body/eval_jaxpr/ppermute | solution.py:24
  242.6 10.4 collective-permute-start.2
  254.6 7.8 collective-permute-start.3
  272.2 11.2 %collective-permute-start.1 = (f32[16,2,1,256]{3,2,1,0:T(1,128)S(1)}, f32[16,2,1,256]{3,2,1,0:T(1,128)S(1)}, u32[]{:S(2)}, u32[]{:S(2)}) collective-permute-start(f32[16,2,1,256]{3,2,1,0:T(1,128)S(1)} %get-tuple-element.793), channel_id=1, source_target_pairs={{1,0},{2,1},{3,2},{4,3},{5,4},{6,5},{7,6},{8,7},{9,8},{10,9},{11,1... | collective-permute-start | bytes 98312 | tf_op jit(solution)/shard_map/while/body/eval_jaxpr/ppermute | solution.py:24
  274.1 10.4 collective-permute-start.2
  286.1 7.8 collective-permute-start.3
  296.3 7.9 collective-permute-start.5
  304.2 10.9 %collective-permute-start.6 = (f32[16,2,1,256]{3,2,0,1:T(1,128)S(1)}, f32[16,2,1,256]{3,2,0,1:T(1,128)S(1)}, u32[]{:S(2)}, u32[]{:S(2)}) collective-permute-start(f32[16,2,1,256]{3,2,0,1:T(1,128)S(1)} %get-tuple-element.816), channel_id=1, source_target_pairs={{1,0},{2,1},{3,2},{4,3},{5,4},{6,5},{7,6},{8,7},{9,8},{10,9},{11,1... | collective-permute-start | bytes 98312 | tf_op jit(solution)/shard_map/while/body/eval_jaxpr/ppermute | solution.py:24
  306.1 10.2 collective-permute-start.7
  317.3 7.8 collective-permute-start.8
  335.1 9.6 collective-permute-start.6
  337.0 8.7 collective-permute-start.7
  346.7 7.7 collective-permute-start.8
  356.7 8.0 collective-permute-start.5
  364.7 9.2 collective-permute-start.6
  366.6 8.2 collective-permute-start.7
  375.8 7.7 collective-permute-start.8
  385.8 8.0 collective-permute-start.5
  393.9 11.3 %collective-permute-start.6 = (f32[16,2,1,256]{3,2,0,1:T(1,128)S(1)}, f32[16,2,1,256]{3,2,0,1:T(1,128)S(1)}, u32[]{:S(2)}, u32[]{:S(2)}) collective-permute-start(f32[16,2,1,256]{3,2,0,1:T(1,128)S(1)} %get-tuple-element.816), channel_id=1, source_target_pairs={{1,0},{2,1},{3,2},{4,3},{5,4},{6,5},{7,6},{8,7},{9,8},{10,9},{11,1... | collective-permute-start | bytes 98312 | tf_op jit(solution)/shard_map/while/body/eval_jaxpr/ppermute | solution.py:24
  395.8 10.4 collective-permute-start.7
  407.3 7.7 collective-permute-start.8
  417.3 8.1 collective-permute-start.5
  425.4 11.9 %collective-permute-start.6 = (f32[16,2,1,256]{3,2,0,1:T(1,128)S(1)}, f32[16,2,1,256]{3,2,0,1:T(1,128)S(1)}, u32[]{:S(2)}, u32[]{:S(2)}) collective-permute-start(f32[16,2,1,256]{3,2,0,1:T(1,128)S(1)} %get-tuple-element.816), channel_id=1, source_target_pairs={{1,0},{2,1},{3,2},{4,3},{5,4},{6,5},{7,6},{8,7},{9,8},{10,9},{11,1... | collective-permute-start | bytes 98312 | tf_op jit(solution)/shard_map/while/body/eval_jaxpr/ppermute | solution.py:24
  427.3 10.9 %collective-permute-start.7 = (f32[16,2,1,256]{3,2,0,1:T(1,128)S(1)}, f32[16,2,1,256]{3,2,0,1:T(1,128)S(1)}, u32[]{:S(2)}, u32[]{:S(2)}) collective-permute-start(f32[16,2,1,256]{3,2,0,1:T(1,128)S(1)} %get-tuple-element.817), channel_id=1, source_target_pairs={{0,1},{1,2},{2,3},{3,4},{4,5},{5,6},{6,7},{7,8},{8,9},{9,10},{10,1... | collective-permute-start | bytes 98312 | tf_op jit(solution)/shard_map/while/body/eval_jaxpr/ppermute | solution.py:23
  439.2 7.7 collective-permute-start.8
  449.2 8.1 collective-permute-start.5
  457.3 11.9 %collective-permute-start.6 = (f32[16,2,1,256]{3,2,0,1:T(1,128)S(1)}, f32[16,2,1,256]{3,2,0,1:T(1,128)S(1)}, u32[]{:S(2)}, u32[]{:S(2)}) collective-permute-start(f32[16,2,1,256]{3,2,0,1:T(1,128)S(1)} %get-tuple-element.816), channel_id=1, source_target_pairs={{1,0},{2,1},{3,2},{4,3},{5,4},{6,5},{7,6},{8,7},{9,8},{10,9},{11,1... | collective-permute-start | bytes 98312 | tf_op jit(solution)/shard_map/while/body/eval_jaxpr/ppermute | solution.py:24
  459.3 10.9 %collective-permute-start.7 = (f32[16,2,1,256]{3,2,0,1:T(1,128)S(1)}, f32[16,2,1,256]{3,2,0,1:T(1,128)S(1)}, u32[]{:S(2)}, u32[]{:S(2)}) collective-permute-start(f32[16,2,1,256]{3,2,0,1:T(1,128)S(1)} %get-tuple-element.817), channel_id=1, source_target_pairs={{0,1},{1,2},{2,3},{3,4},{4,5},{5,6},{6,7},{7,8},{8,9},{9,10},{10,1... | collective-permute-start | bytes 98312 | tf_op jit(solution)/shard_map/while/body/eval_jaxpr/ppermute | solution.py:23
  471.2 7.7 collective-permute-start.8
  481.2 8.1 collective-permute-start.5
  489.3 11.9 %collective-permute-start.6 = (f32[16,2,1,256]{3,2,0,1:T(1,128)S(1)}, f32[16,2,1,256]{3,2,0,1:T(1,128)S(1)}, u32[]{:S(2)}, u32[]{:S(2)}) collective-permute-start(f32[16,2,1,256]{3,2,0,1:T(1,128)S(1)} %get-tuple-element.816), channel_id=1, source_target_pairs={{1,0},{2,1},{3,2},{4,3},{5,4},{6,5},{7,6},{8,7},{9,8},{10,9},{11,1... | collective-permute-start | bytes 98312 | tf_op jit(solution)/shard_map/while/body/eval_jaxpr/ppermute | solution.py:24
  491.3 10.9 %collective-permute-start.7 = (f32[16,2,1,256]{3,2,0,1:T(1,128)S(1)}, f32[16,2,1,256]{3,2,0,1:T(1,128)S(1)}, u32[]{:S(2)}, u32[]{:S(2)}) collective-permute-start(f32[16,2,1,256]{3,2,0,1:T(1,128)S(1)} %get-tuple-element.817), channel_id=1, source_target_pairs={{0,1},{1,2},{2,3},{3,4},{4,5},{5,6},{6,7},{7,8},{8,9},{9,10},{10,1... | collective-permute-start | bytes 98312 | tf_op jit(solution)/shard_map/while/body/eval_jaxpr/ppermute | solution.py:23
  503.2 7.7 collective-permute-start.8
  513.2 8.1 collective-permute-start.5
  521.3 10.9 %collective-permute-start.6 = (f32[16,2,1,256]{3,2,0,1:T(1,128)S(1)}, f32[16,2,1,256]{3,2,0,1:T(1,128)S(1)}, u32[]{:S(2)}, u32[]{:S(2)}) collective-permute-start(f32[16,2,1,256]{3,2,0,1:T(1,128)S(1)} %get-tuple-element.816), channel_id=1, source_target_pairs={{1,0},{2,1},{3,2},{4,3},{5,4},{6,5},{7,6},{8,7},{9,8},{10,9},{11,1... | collective-permute-start | bytes 98312 | tf_op jit(solution)/shard_map/while/body/eval_jaxpr/ppermute | solution.py:24
  523.3 9.9 collective-permute-start.7
  534.2 7.7 collective-permute-start.8
  548.8 9.8 collective-permute-start.17
  558.8 20.0 %collective-permute-start.18 = (f32[16,2,4,1,256]{4,3,2,0,1:T(1,128)S(1)}, f32[16,2,4,1,256]{4,3,2,0,1:T(1,128)S(1)}, u32[]{:S(2)}, u32[]{:S(2)}) collective-permute-start(f32[16,2,4,1,256]{4,3,2,0,1:T(1,128)S(1)} %get-tuple-element.649), channel_id=1, source_target_pairs={{0,1},{1,2},{2,3},{3,4},{4,5},{5,6},{6,7},{7,8},{8,9},{9,10},{10,1... | collective-permute-start | bytes 393224 | tf_op jit(solution)/shard_map/ppermute | solution.py:23
  568.5 10.3 collective-permute-start.19
  591.8 8.2 collective-permute-start.21
  (46 other events, 630.1 us)
Sparse Core Ops, SparseCore 0:
  585.5 472.4 all-gather.2
